TPU v7x, 32 devices: a whole 2x2x4 slice. The times are simulated.
32 devices in a mesh: dp: 16 (over z, y, core), tensor: 2 (over x).
Axes of the slice: x: 2, y: 2, z: 4, core: 2. Of those that a mesh axis runs over, the one named last changes fastest.
Arguments:
- layer_input: bfloat16 [32768, 1024], P(('dp', 'tensor')), may hold values from -6 to 6
- target: bfloat16 [32768, 1024], P(('dp', 'tensor')), may hold values from -6 to 6
- segment: int32 [32768], P('dp'), may hold values from 0 to 2047, as said below
- pad_mask: int32 [32768], P(('dp', 'tensor')), may hold values from 0 to 1, as said below
- norm1_gain: float32 [1024], replicated, may hold values from 0.5 to 1.5
- w_query: bfloat16 [1024, 1024], P('dp', 'tensor'), may hold values from -0.1875 to 0.1875
- w_key: bfloat16 [1024, 1024], P('dp', 'tensor'), may hold values from -0.1875 to 0.1875
- w_value: bfloat16 [1024, 2048], P('dp', 'tensor'), may hold values from -0.1875 to 0.1875
- w_gate_out: bfloat16 [1024, 2048], P('dp', 'tensor'), may hold values from -0.1875 to 0.1875
- w_decay: bfloat16 [1024, 8], P('dp', 'tensor'), may hold values from -0.1875 to 0.1875
- w_beta: bfloat16 [1024, 8], P('dp', 'tensor'), may hold values from -0.1875 to 0.1875
- conv_query: float32 [4, 1024], replicated, may hold values from -3 to 3
- conv_key: float32 [4, 1024], replicated, may hold values from -3 to 3
- conv_value: float32 [4, 2048], replicated, may hold values from -3 to 3
- decay_scale: float32 [8], replicated, may hold values from 0.3 to 8
- decay_bias: float32 [8], replicated, may hold values from -5 to -2
- out_norm_gain: float32 [256], replicated, may hold values from 0.5 to 1.5
- w_out: bfloat16 [1024, 2048], P('dp', 'tensor'), may hold values from -0.25 to 0.25
- norm2_gain: float32 [1024], replicated, may hold values from 0.5 to 1.5
- w_ffn_gate: bfloat16 [1024, 2816], P('dp', 'tensor'), may hold values from -0.1875 to 0.1875
- w_ffn_up: bfloat16 [1024, 2816], P('dp', 'tensor'), may hold values from -0.1875 to 0.1875
- w_ffn_down: bfloat16 [1024, 2816], P('dp', 'tensor'), may hold values from -0.109375 to 0.109375
Outputs:
- output: float32 [32768, 1024], P(('dp', 'tensor'))
- loss: float32 [], replicated
- grad_input: float32 [32768, 1024], P(('dp', 'tensor'))
- grad_norm1_gain: float32 [1024], replicated
- grad_w_query: float32 [1024, 1024], P('dp', 'tensor')
- grad_w_key: float32 [1024, 1024], P('dp', 'tensor')
- grad_w_value: float32 [1024, 2048], P('dp', 'tensor')
- grad_w_gate_out: float32 [1024, 2048], P('dp', 'tensor')
- grad_w_decay: float32 [1024, 8], P('dp', 'tensor')
- grad_w_beta: float32 [1024, 8], P('dp', 'tensor')
- grad_conv_query: float32 [4, 1024], replicated
- grad_conv_key: float32 [4, 1024], replicated
- grad_conv_value: float32 [4, 2048], replicated
- grad_decay_scale: float32 [8], replicated
- grad_decay_bias: float32 [8], replicated
- grad_out_norm_gain: float32 [256], replicated
- grad_w_out: float32 [1024, 2048], P('dp', 'tensor')
- grad_norm2_gain: float32 [1024], replicated
- grad_w_ffn_gate: float32 [1024, 2816], P('dp', 'tensor')
- grad_w_ffn_up: float32 [1024, 2816], P('dp', 'tensor')
- grad_w_ffn_down: float32 [1024, 2816], P('dp', 'tensor')
Inputs may be any that keep to these rules, and one draw needn't show every extreme that they name: `segment`: ids never decrease within a sequence of 1024 tokens; each document's tokens share one id, the padding at a sequence's end has an id of its own, and different sequences share no id. Documents have 1 to 800 tokens, the last of a sequence cut to fit. `pad_mask`: each sequence of 1024 tokens ends with 1 to max(64, 2) padding tokens, marked 0; all other tokens are 1.
All inputs are finite; a program needn't handle non-finite values.
Results may differ from a plain program's by a relative error of at most 0.015.
Values may be sent and summed in bfloat16 or wider, within the bound.
No kernel may reach another device: no remote copies, remote signals or barrier semaphores. Data moves between devices by JAX's collectives and lax.ppermute only.
A program may use at most 384 MiB of HBM per device.

v0:
```python
import jax
import jax.numpy as jnp
from jax import lax
from jax.sharding import PartitionSpec as P

CH = 64
LENGTH = 1024
exact_precision = lax.Precision.HIGHEST


def rms_scale(values, gain):
    return values * lax.rsqrt(jnp.mean(values * values, axis=-1, keepdims=True) + 1e-06) * gain


def shift_masks(segment_ids, taps):
    masks = [jnp.ones(segment_ids.shape, jnp.float32)]
    for offset in range(1, taps):
        earlier = jnp.concatenate([jnp.full((offset,), -1, jnp.int32), segment_ids[:-offset]])
        masks.append((segment_ids == earlier).astype(jnp.float32))
    return masks


def short_conv(values, kernel, masks):
    result = values * kernel[0]
    for offset in range(1, len(masks)):
        shifted = jnp.concatenate(
            [jnp.zeros((offset, values.shape[1]), jnp.float32), values[:-offset]]
        )
        result = result + shifted * masks[offset][:, None] * kernel[offset]
    return result


def unit_rows(values):
    return values * lax.rsqrt(jnp.sum(values * values, axis=-1, keepdims=True) + 1e-06)


def lower_inverse(lower_part, length):
    negative = -lower_part
    inverse = jnp.eye(length, dtype=jnp.float32) + negative
    power = negative
    covered = 2
    while covered < length:
        power = jnp.einsum("hij,hjk->hik", power, power, precision=exact_precision)
        inverse = inverse + jnp.einsum("hij,hjk->hik", inverse, power, precision=exact_precision)
        covered = covered * 2
    return inverse


def block_update(state, inputs):
    queries, keys, values, betas, log_decay, seg_block, previous = inputs
    length = queries.shape[0]
    cumulative = jnp.cumsum(log_decay, axis=0)
    order = jnp.arange(length)
    causal = order[:, None] >= order[None, :]
    strict = order[:, None] > order[None, :]
    same_doc = seg_block[:, None] == seg_block[None, :]
    visible = (same_doc & causal)[:, :, None]
    spread = cumulative[:, None, :] - cumulative[None, :, :]
    weights = jnp.where(visible, jnp.exp(jnp.where(visible, spread, 0.0)), 0.0)
    carried = (seg_block == previous).astype(jnp.float32)
    carry_decay = jnp.exp(cumulative) * carried[:, None]
    key_gram = jnp.einsum("ihd,jhd->ijh", keys, keys, precision=exact_precision)
    lower_part = jnp.where(strict[:, :, None], betas[:, None, :] * weights * key_gram, 0.0)
    inverse = lower_inverse(jnp.transpose(lower_part, (2, 0, 1)), length)
    key_state = jnp.einsum("ihd,hde->ihe", keys, state, precision=exact_precision)
    target_rows = betas[:, :, None] * (values - carry_decay[:, :, None] * key_state)
    pseudo = jnp.einsum("hij,jhe->hie", inverse, target_rows, precision=exact_precision)
    scores = jnp.einsum("ihd,jhd->hij", queries, keys, precision=exact_precision) * jnp.transpose(
        weights, (2, 0, 1)
    )
    query_state = jnp.einsum("ihd,hde->ihe", queries, state, precision=exact_precision)
    outputs = carry_decay[:, :, None] * query_state + jnp.einsum(
        "hij,hje->ihe", scores, pseudo, precision=exact_precision
    )
    last_weights = weights[-1]
    new_state = (carried[-1] * jnp.exp(cumulative[-1]))[:, None, None] * state + jnp.einsum(
        "jh,jhd,hje->hde", last_weights, keys, pseudo, precision=exact_precision
    )
    return (new_state, outputs)


def mixer_sequence(
    q_pre,
    k_pre,
    v_pre,
    g_pre,
    a_pre,
    b_pre,
    segment_ids,
    conv_q,
    conv_k,
    conv_v,
    scale_rate,
    bias_rate,
    out_gain,
):
    length = q_pre.shape[0]
    heads = a_pre.shape[1]
    key_size = q_pre.shape[1] // heads
    value_size = v_pre.shape[1] // heads
    masks = shift_masks(segment_ids, conv_q.shape[0])
    queries = unit_rows(
        jax.nn.silu(short_conv(q_pre, conv_q, masks)).reshape(length, heads, key_size)
    ) * key_size ** (-0.5)
    keys = unit_rows(jax.nn.silu(short_conv(k_pre, conv_k, masks)).reshape(length, heads, key_size))
    values = jax.nn.silu(short_conv(v_pre, conv_v, masks)).reshape(length, heads, value_size)
    betas = jax.nn.sigmoid(b_pre)
    log_decay = -scale_rate * jax.nn.softplus(a_pre + bias_rate)
    blocks = length // CH
    seg_blocks = segment_ids.reshape(blocks, CH)
    previous = jnp.concatenate([jnp.full((1,), -1, jnp.int32), seg_blocks[:-1, -1]])
    state = jnp.zeros((heads, key_size, value_size), jnp.float32)
    carried_in = (
        queries.reshape(blocks, CH, heads, key_size),
        keys.reshape(blocks, CH, heads, key_size),
        values.reshape(blocks, CH, heads, value_size),
        betas.reshape(blocks, CH, heads),
        log_decay.reshape(blocks, CH, heads),
        seg_blocks,
        previous,
    )
    final_state, outputs = lax.scan(jax.checkpoint(block_update), state, carried_in)
    outputs = outputs.reshape(length, heads, value_size)
    gated = rms_scale(outputs, out_gain) * jax.nn.silu(g_pre.reshape(length, heads, value_size))
    return gated.reshape(length, heads * value_size)


def contract_rows(left, right):
    return lax.dot_general(
        left, right, (((0,), (0,)), ((), ())), preferred_element_type=jnp.float32
    )


def contract_cols(left, right):
    return lax.dot_general(
        left, right, (((1,), (1,)), ((), ())), preferred_element_type=jnp.float32
    )


def feed_inputs(normed_rows, gate_weight, up_weight):
    gate_pre = jnp.dot(normed_rows, gate_weight, preferred_element_type=jnp.float32)
    up_pre = jnp.dot(normed_rows, up_weight, preferred_element_type=jnp.float32)
    return (gate_pre, up_pre)


def on_device(
    layer_input,
    target,
    segment,
    pad_mask,
    norm1_gain,
    w_query,
    w_key,
    w_value,
    w_gate_out,
    w_decay,
    w_beta,
    conv_query,
    conv_key,
    conv_value,
    decay_scale,
    decay_bias,
    out_norm_gain,
    w_out,
    norm2_gain,
    w_ffn_gate,
    w_ffn_up,
    w_ffn_down,
):
    own_rows, width = layer_input.shape
    group_rows = segment.shape[0]
    sequences = group_rows // LENGTH
    tensor_index = lax.axis_index("tensor")
    heads_local = w_decay.shape[1]
    query_cols = w_query.shape[1]
    value_cols = w_value.shape[1]
    input_float = layer_input.astype(jnp.float32)
    normed_own, norm1_pull = jax.vjp(rms_scale, input_float, norm1_gain)
    normed = lax.all_gather(normed_own.astype(jnp.bfloat16), "tensor", axis=0, tiled=True)
    full_query, full_key, full_value, full_gate, full_decay, full_beta, full_out = (
        lax.all_gather(w_query, "dp", axis=0, tiled=True),
        lax.all_gather(w_key, "dp", axis=0, tiled=True),
        lax.all_gather(w_value, "dp", axis=0, tiled=True),
        lax.all_gather(w_gate_out, "dp", axis=0, tiled=True),
        lax.all_gather(w_decay, "dp", axis=0, tiled=True),
        lax.all_gather(w_beta, "dp", axis=0, tiled=True),
        lax.all_gather(w_out, "dp", axis=0, tiled=True),
    )
    proj_weights = (full_query, full_key, full_value, full_gate, full_decay, full_beta)
    projected = [
        jnp.dot(normed, weight, preferred_element_type=jnp.float32) for weight in proj_weights
    ]
    conv_q_local = lax.dynamic_slice_in_dim(conv_query, tensor_index * query_cols, query_cols, 1)
    conv_k_local = lax.dynamic_slice_in_dim(conv_key, tensor_index * query_cols, query_cols, 1)
    conv_v_local = lax.dynamic_slice_in_dim(conv_value, tensor_index * value_cols, value_cols, 1)
    scale_local = lax.dynamic_slice_in_dim(decay_scale, tensor_index * heads_local, heads_local, 0)
    bias_local = lax.dynamic_slice_in_dim(decay_bias, tensor_index * heads_local, heads_local, 0)
    seg_rows = segment.reshape(sequences, LENGTH)

    def mixer_local(
        q_pre,
        k_pre,
        v_pre,
        g_pre,
        a_pre,
        b_pre,
        conv_q,
        conv_k,
        conv_v,
        scale_rate,
        bias_rate,
        out_gain,
    ):
        shaped = [
            item.reshape(sequences, LENGTH, item.shape[1])
            for item in (q_pre, k_pre, v_pre, g_pre, a_pre, b_pre)
        ]
        mixed_rows = jax.vmap(
            mixer_sequence, in_axes=(0, 0, 0, 0, 0, 0, 0, None, None, None, None, None, None)
        )(*shaped, seg_rows, conv_q, conv_k, conv_v, scale_rate, bias_rate, out_gain)
        return mixed_rows.reshape(group_rows, mixed_rows.shape[2])

    mixed, mixer_pull = jax.vjp(
        mixer_local,
        *projected,
        conv_q_local,
        conv_k_local,
        conv_v_local,
        scale_local,
        bias_local,
        out_norm_gain
    )
    mixed_low = mixed.astype(jnp.bfloat16)
    attention = lax.psum_scatter(
        contract_cols(mixed_low, full_out), "tensor", scatter_dimension=0, tiled=True
    )
    residual = input_float + attention
    normed2_own, norm2_pull = jax.vjp(rms_scale, residual, norm2_gain)
    normed2 = lax.all_gather(normed2_own.astype(jnp.bfloat16), "tensor", axis=0, tiled=True)
    ffn_gate_w, ffn_up_w, ffn_down_w = (
        lax.all_gather(w_ffn_gate, "dp", axis=0, tiled=True),
        lax.all_gather(w_ffn_up, "dp", axis=0, tiled=True),
        lax.all_gather(w_ffn_down, "dp", axis=0, tiled=True),
    )
    gate_pre, up_pre = feed_inputs(normed2, ffn_gate_w, ffn_up_w)
    hidden = (jax.nn.silu(gate_pre) * up_pre).astype(jnp.bfloat16)
    ffn_out = lax.psum_scatter(
        contract_cols(hidden, ffn_down_w).astype(jnp.bfloat16),
        "tensor",
        scatter_dimension=0,
        tiled=True,
    ).astype(jnp.float32)
    output = residual + ffn_out
    live = pad_mask.astype(jnp.float32)
    error = output - target.astype(jnp.float32)
    loss_sum, count = lax.psum(
        (jnp.sum(live[:, None] * error * error), jnp.sum(live)), ("dp", "tensor")
    )
    loss = loss_sum / (count * width)
    all_tokens = own_rows * lax.axis_size("dp") * lax.axis_size("tensor")
    grad_output = error * live[:, None] * (all_tokens / count)
    grad_ffn = lax.all_gather(grad_output.astype(jnp.bfloat16), "tensor", axis=0, tiled=True)
    grad_hidden = jnp.dot(grad_ffn, ffn_down_w, preferred_element_type=jnp.float32)
    sigmoid_gate = jax.nn.sigmoid(gate_pre)
    grad_gate = (
        grad_hidden * up_pre * sigmoid_gate * (1.0 + gate_pre * (1.0 - sigmoid_gate))
    ).astype(jnp.bfloat16)
    grad_up = (grad_hidden * gate_pre * sigmoid_gate).astype(jnp.bfloat16)
    grad_down_local = contract_rows(grad_ffn, hidden)
    grad_gate_local = contract_rows(normed2, grad_gate)
    grad_up_local = contract_rows(normed2, grad_up)
    normed2_part = contract_cols(grad_gate, ffn_gate_w) + contract_cols(grad_up, ffn_up_w)
    grad_normed2 = lax.psum_scatter(
        normed2_part.astype(jnp.bfloat16), "tensor", scatter_dimension=0, tiled=True
    ).astype(jnp.float32)
    grad_residual_norm, grad_gain_two = norm2_pull(grad_normed2)
    grad_residual = grad_output + grad_residual_norm
    grad_attention = lax.all_gather(
        grad_residual.astype(jnp.bfloat16), "tensor", axis=0, tiled=True
    )
    grad_mixed = jnp.dot(grad_attention, full_out, preferred_element_type=jnp.float32)
    grad_out_local = contract_rows(grad_attention, mixed_low)
    mixer_grads = mixer_pull(grad_mixed)
    pre_grads = [item.astype(jnp.bfloat16) for item in mixer_grads[:6]]
    normed_part = contract_cols(pre_grads[0], full_query)
    for grad_item, weight in zip(pre_grads[1:], proj_weights[1:]):
        normed_part = normed_part + contract_cols(grad_item, weight)
    weight_locals = [contract_rows(normed, grad_item) for grad_item in pre_grads]
    grad_normed = lax.psum_scatter(
        normed_part.astype(jnp.bfloat16), "tensor", scatter_dimension=0, tiled=True
    ).astype(jnp.float32)
    grad_input_norm, grad_gain_one = norm1_pull(grad_normed)
    grad_input = grad_residual + grad_input_norm
    owned = (
        lax.psum_scatter(
            grad_gate_local.astype(jnp.bfloat16), "dp", scatter_dimension=0, tiled=True
        ).astype(jnp.float32),
        lax.psum_scatter(
            grad_up_local.astype(jnp.bfloat16), "dp", scatter_dimension=0, tiled=True
        ).astype(jnp.float32),
        lax.psum_scatter(
            grad_down_local.astype(jnp.bfloat16), "dp", scatter_dimension=0, tiled=True
        ).astype(jnp.float32),
        lax.psum_scatter(
            weight_locals[0].astype(jnp.bfloat16), "dp", scatter_dimension=0, tiled=True
        ).astype(jnp.float32),
        lax.psum_scatter(
            weight_locals[1].astype(jnp.bfloat16), "dp", scatter_dimension=0, tiled=True
        ).astype(jnp.float32),
        lax.psum_scatter(
            weight_locals[2].astype(jnp.bfloat16), "dp", scatter_dimension=0, tiled=True
        ).astype(jnp.float32),
        lax.psum_scatter(
            weight_locals[3].astype(jnp.bfloat16), "dp", scatter_dimension=0, tiled=True
        ).astype(jnp.float32),
        lax.psum_scatter(
            weight_locals[4].astype(jnp.bfloat16), "dp", scatter_dimension=0, tiled=True
        ).astype(jnp.float32),
        lax.psum_scatter(
            weight_locals[5].astype(jnp.bfloat16), "dp", scatter_dimension=0, tiled=True
        ).astype(jnp.float32),
        lax.psum_scatter(
            grad_out_local.astype(jnp.bfloat16), "dp", scatter_dimension=0, tiled=True
        ).astype(jnp.float32),
    )
    conv_q_full = lax.dynamic_update_slice_in_dim(
        jnp.zeros_like(conv_query), mixer_grads[6], tensor_index * query_cols, 1
    )
    conv_k_full = lax.dynamic_update_slice_in_dim(
        jnp.zeros_like(conv_key), mixer_grads[7], tensor_index * query_cols, 1
    )
    conv_v_full = lax.dynamic_update_slice_in_dim(
        jnp.zeros_like(conv_value), mixer_grads[8], tensor_index * value_cols, 1
    )
    scale_full = lax.dynamic_update_slice_in_dim(
        jnp.zeros_like(decay_scale), mixer_grads[9], tensor_index * heads_local, 0
    )
    bias_full = lax.dynamic_update_slice_in_dim(
        jnp.zeros_like(decay_bias), mixer_grads[10], tensor_index * heads_local, 0
    )
    summed = lax.psum(
        (
            grad_gain_one,
            grad_gain_two,
            conv_q_full,
            conv_k_full,
            conv_v_full,
            scale_full,
            bias_full,
            mixer_grads[11],
        ),
        ("dp", "tensor"),
    )
    return (
        output,
        loss,
        grad_input,
        summed[0],
        owned[3],
        owned[4],
        owned[5],
        owned[6],
        owned[7],
        owned[8],
        summed[2],
        summed[3],
        summed[4],
        summed[5],
        summed[6],
        summed[7],
        owned[9],
        summed[1],
        owned[0],
        owned[1],
        owned[2],
    )


def solution(mesh):
    return jax.shard_map(
        on_device,
        mesh=mesh,
        in_specs=(
            P(("dp", "tensor"), None),
            P(("dp", "tensor"), None),
            P("dp"),
            P(("dp", "tensor")),
            P(),
            P("dp", "tensor"),
            P("dp", "tensor"),
            P("dp", "tensor"),
            P("dp", "tensor"),
            P("dp", "tensor"),
            P("dp", "tensor"),
            P(),
            P(),
            P(),
            P(),
            P(),
            P(),
            P("dp", "tensor"),
            P(),
            P("dp", "tensor"),
            P("dp", "tensor"),
            P("dp", "tensor"),
        ),
        out_specs=(
            P(("dp", "tensor"), None),
            P(),
            P(("dp", "tensor"), None),
            P(),
            P("dp", "tensor"),
            P("dp", "tensor"),
            P("dp", "tensor"),
            P("dp", "tensor"),
            P("dp", "tensor"),
            P("dp", "tensor"),
            P(),
            P(),
            P(),
            P(),
            P(),
            P(),
            P("dp", "tensor"),
            P(),
            P("dp", "tensor"),
            P("dp", "tensor"),
            P("dp", "tensor"),
        ),
        check_vma=False,
    )
```

profile of v0, /device:TPU:0, one launch (start us, length us, event | category | flops | bytes accessed | tf_op | source)
XLA Modules:
  0.0 3118.4 jit_solution(9823898228020338124)
XLA Ops:
  17.5 23.1 all-gather
  60.5 48.3 %all-gather.15.cloned.1.call-done = bf16[2048,1024]{1,0:T(8,128)(2,1)} async-done(((bf16[1024,1024]{1,0:T(8,128)(2,1)}), bf16[2048,1024]{1,0:T(8,128)(2,1)}) %all-gather.15.cloned.1.call-update) | async-done | bytes 4194320 | tf_op jit(solution)/shard_map/all_gather | solution.py:179
  115.6 33.3 %all-gather.17.cloned.1.call-done = bf16[1024,512]{1,0:T(8,128)(2,1)} async-done(((bf16[64,512]{1,0:T(8,128)(2,1)}), bf16[1024,512]{1,0:T(8,128)(2,1)}) %all-gather.17.cloned.1.call-update) | async-done | bytes 1048592 | tf_op jit(solution)/shard_map/all_gather | solution.py:182
  267.7 323.5 %while.42 = (s32[]{:T(128)}, f32[2,4,128,256]{3,2,1,0:T(8,128)S(1)}, f32[16,2,64,4,256]{4,2,3,1,0:T(8,128)}, f32[16,2,4,128,256]{4,3,2,1,0:T(8,128)}, s32[16,2,6...) while((s32[]{:T(128)}, ...), condition=%wide.region_5.6_spmd.clone, body=%wide.region_3.5_spmd.clone.sunk | while | flops 1160541952 | bytes 16545918 | solution.py:122
  627.4 18.5 multiply_convert_fusion.3
  657.4 97.5 %reduce-scatter.19.cloned.1.call-done = f32[1024,1024]{1,0:T(8,128)} async-done(((f32[2048,1024]{1,0:T(8,128)}), f32[1024,1024]{1,0:T(8,128)}) %reduce-scatter.19.cloned.1.call-update) | async-done | bytes 4194320 | tf_op jit(solution)/shard_map/reduce_scatter | solution.py:234
  762.9 38.9 %all-gather.29.cloned.1.call-done = bf16[1024,1408]{1,0:T(8,128)(2,1)} async-done(((bf16[64,1408]{1,0:T(8,128)(2,1)}), bf16[1024,1408]{1,0:T(8,128)(2,1)}) %all-gather.29.cloned.1.call-update) | async-done | bytes 2883600 | tf_op jit(solution)/shard_map/all_gather | solution.py:241
  801.9 57.3 %all-gather.27.cloned.1.call-done = bf16[2048,1024]{1,0:T(8,128)(2,1)} async-done(((bf16[1024,1024]{1,0:T(8,128)(2,1)}), bf16[2048,1024]{1,0:T(8,128)(2,1)}) %all-gather.27.cloned.1.call-update) | async-done | bytes 4194320 | tf_op jit(solution)/shard_map/all_gather | solution.py:239
  871.1 34.9 %all-gather.31.cloned.1.call-done = bf16[1024,1408]{1,0:T(8,128)(2,1)} async-done(((bf16[64,1408]{1,0:T(8,128)(2,1)}), bf16[1024,1408]{1,0:T(8,128)(2,1)}) %all-gather.31.cloned.1.call-update) | async-done | bytes 2883600 | tf_op jit(solution)/shard_map/all_gather | solution.py:242
  920.8 30.5 all-gather.33.cloned.1.call-done
  963.9 39.9 %psum.71 = f32[]{:T(128)} all-reduce(f32[]{:T(128)} %convert_reduce_fusion), channel_id=1, replica_groups=mesh['dp'=16,'tensor'=2] {'dp','tensor'}, use_global_device_ids=true, to_apply=%region_13.14 | all-reduce | flops 1 | bytes 8 | tf_op jit(solution)/shard_map/psum | solution.py:256
  1023.3 56.7 %all-gather.35.cloned.1.call-done = bf16[2048,1024]{1,0:T(8,128)(2,1)} async-done(((bf16[1024,1024]{1,0:T(8,128)(2,1)}), bf16[2048,1024]{1,0:T(8,128)(2,1)}) %all-gather.35.cloned.1.call-update) | async-done | bytes 4194320 | tf_op jit(solution)/shard_map/all_gather | solution.py:262
  1080.0 19.6 multiply_convert_fusion
  1117.0 54.4 %reduce-scatter.23.cloned.1.call-done = bf16[1024,1024]{1,0:T(8,128)(2,1)} async-done(((bf16[2048,1024]{1,0:T(8,128)(2,1)}), bf16[1024,1024]{1,0:T(8,128)(2,1)}) %reduce-scatter.23.cloned.1.call-update) | async-done | bytes 2097168 | tf_op jit(solution)/shard_map/reduce_scatter | solution.py:273
  1240.9 18.8 fusion.145
  1302.2 1161.9 %while.43 = (s32[]{:T(128)}, f32[2,4,128,256]{3,2,1,0:T(8,128)}, f32[16,2,64,4,128]{4,2,3,1,0:T(8,128)}, f32[16,2,64,4,128]{4,2,3,1,0:T(8,128)}, f32[16,2,64,4,2...) while((s32[]{:T(128)}, f32[2,4,128,256]{3,2,1,0:T(8,128)}, ...), condition=%wide.region_27.28_spmd.clone, body=%wide.region_17.27_spmd.clone.sunk | while | flops 3179373312 | bytes 74722920 | solution.py:122
  2534.9 28.9 multiply_reduce_fusion.18
  2631.3 25.2 multiply_reduce_fusion.8
  2768.9 42.1 %reduce-scatter.27.cloned.1.call-done = bf16[64,512]{1,0:T(8,128)(2,1)} async-done(((bf16[1024,512]{1,0:T(8,128)(2,1)}), bf16[64,512]{1,0:T(8,128)(2,1)}) %reduce-scatter.27.cloned.1.call-update) | async-done | bytes 65552 | tf_op jit(solution)/shard_map/reduce_scatter | solution.py:304
  2812.6 62.8 %reduce-scatter.35.cloned.1.call-done = bf16[64,1024]{1,0:T(8,128)(2,1)} async-done(((bf16[1024,1024]{1,0:T(8,128)(2,1)}), bf16[64,1024]{1,0:T(8,128)(2,1)}) %reduce-scatter.35.cloned.1.call-update) | async-done | bytes 131088 | tf_op jit(solution)/shard_map/reduce_scatter | solution.py:322
  2877.0 63.1 %reduce-scatter.31.cloned.1.call-done = bf16[64,1024]{1,0:T(8,128)(2,1)} async-done(((bf16[1024,1024]{1,0:T(8,128)(2,1)}), bf16[64,1024]{1,0:T(8,128)(2,1)}) %reduce-scatter.31.cloned.1.call-update) | async-done | bytes 131088 | tf_op jit(solution)/shard_map/reduce_scatter | solution.py:310
  2941.6 62.7 %reduce-scatter.33.cloned.1.call-done = bf16[64,1024]{1,0:T(8,128)(2,1)} async-done(((bf16[1024,1024]{1,0:T(8,128)(2,1)}), bf16[64,1024]{1,0:T(8,128)(2,1)}) %reduce-scatter.33.cloned.1.call-update) | async-done | bytes 131088 | tf_op jit(solution)/shard_map/reduce_scatter | solution.py:313
  3005.9 54.5 %reduce-scatter.25.cloned.1.call-done = bf16[1024,1024]{1,0:T(8,128)(2,1)} async-done(((bf16[2048,1024]{1,0:T(8,128)(2,1)}), bf16[1024,1024]{1,0:T(8,128)(2,1)}) %reduce-scatter.25.cloned.1.call-update) | async-done | bytes 2097168 | tf_op jit(solution)/shard_map/reduce_scatter | solution.py:289
  3063.8 41.1 %all-reduce.38 = (f32[]{:T(128)}, f32[1024]{0:T(1024)}, f32[4,1024]{1,0:T(4,128)}, f32[4,1024]{1,0:T(4,128)}, f32[4,2048]{1,0:T(4,128)}, /*index=5*/f32[8]{0:T(128)}, f32[8]{0:T(128)}, f32[256]{0:T(256)}, f32[1024]{0:T(1024)}) all-reduce(f32[]{:T(128)} %get-tuple-element.925, ...), channel_id=1, replica_groups=mesh['dp'=16,'tensor'=2] {'dp','tensor'}, use_global_device_ids=true, to_apply=%region_11.12 | all-reduce | flops 18705 | bytes 149640 | tf_op jit(solution)/shard_map/psum | solution.py:256
  (3573 shorter events, 2104.9 us)
Async XLA Ops:
  14.8 134.1 %all-gather.17.cloned.1.call-start = ((), (), s32[]{:S(2)}) async-start(), calls=%async_computation.15 | async-start | bytes 1114112 | tf_op jit(solution)/shard_map/all_gather | solution.py:182
  15.6 203.2 %all-gather.19.cloned.1.call-start = ((), (), s32[]{:S(2)}) async-start(), calls=%async_computation.16 | async-start | bytes 2228224 | tf_op jit(solution)/shard_map/all_gather | solution.py:183
  16.1 611.3 %all-gather.23.cloned.1.call-start = ((), (), s32[]{:S(2)}) async-start(), calls=%async_computation.18 | async-start | bytes 2228224 | tf_op jit(solution)/shard_map/all_gather | solution.py:184
  16.7 629.1 %all-gather.25.cloned.1.call-start = ((), (), s32[]{:S(2)}) async-start(), calls=%async_computation.19 | async-start | bytes 2228224 | tf_op jit(solution)/shard_map/all_gather | solution.py:187
  17.3 737.6 %reduce-scatter.19.cloned.1.call-start = ((), (), s32[]{:S(2)}) async-start(), calls=%async_computation.20 | async-start | bytes 12582912 | tf_op jit(solution)/shard_map/reduce_scatter | solution.py:234
  656.6 145.2 %all-gather.29.cloned.1.call-start = ((), (), s32[]{:S(2)}) async-start(), calls=%async_computation.22 | async-start | bytes 3063808 | tf_op jit(solution)/shard_map/all_gather | solution.py:241
  657.4 201.8 %all-gather.27.cloned.1.call-start = ((), (), s32[]{:S(2)}) async-start(), calls=%async_computation.21 | async-start | bytes 6291456 | tf_op jit(solution)/shard_map/all_gather | solution.py:239
  761.6 144.4 %all-gather.31.cloned.1.call-start = ((), (), s32[]{:S(2)}) async-start(), calls=%async_computation.23 | async-start | bytes 3063808 | tf_op jit(solution)/shard_map/all_gather | solution.py:242
  762.2 189.1 %all-gather.33.cloned.1.call-start = ((), (), s32[]{:S(2)}) async-start(), calls=%async_computation.24 | async-start | bytes 3063808 | tf_op jit(solution)/shard_map/all_gather | solution.py:243
  762.9 253.9 %reduce-scatter.21.cloned.1.call-start = ((), (), s32[]{:S(2)}) async-start(), calls=%async_computation.25 | async-start | bytes 6291456 | tf_op jit(solution)/shard_map/reduce_scatter | solution.py:247
  962.6 117.4 %all-gather.35.cloned.1.call-start = ((), (), s32[]{:S(2)}) async-start(), calls=%async_computation.26 | async-start | bytes 6291456 | tf_op jit(solution)/shard_map/all_gather | solution.py:262
  1023.3 148.1 %reduce-scatter.23.cloned.1.call-start = ((), (), s32[]{:S(2)}) async-start(), calls=%async_computation.27 | async-start | bytes 6291456 | tf_op jit(solution)/shard_map/reduce_scatter | solution.py:273
  1116.9 124.0 %all-gather.37.cloned.1.call-start = ((), (), s32[]{:S(2)}) async-start(), calls=%async_computation.28 | async-start | bytes 6291456 | tf_op jit(solution)/shard_map/all_gather | solution.py:278
  1183.8 1572.7 %reduce-scatter.41.cloned.1.call-start = ((), (), s32[]{:S(2)}) async-start(), calls=%async_computation.37 | async-start | bytes 3063808 | tf_op jit(solution)/shard_map/reduce_scatter | solution.py:301
  1195.8 1562.6 %reduce-scatter.37.cloned.1.call-start = ((), (), s32[]{:S(2)}) async-start(), calls=%async_computation.35 | async-start | bytes 3063808 | tf_op jit(solution)/shard_map/reduce_scatter | solution.py:295
  1207.3 1552.7 %reduce-scatter.39.cloned.1.call-start = ((), (), s32[]{:S(2)}) async-start(), calls=%async_computation.36 | async-start | bytes 3063808 | tf_op jit(solution)/shard_map/reduce_scatter | solution.py:298
  1240.8 1523.8 %reduce-scatter.43.cloned.1.call-start = ((), (), s32[]{:S(2)}) async-start(), calls=%async_computation.38 | async-start | bytes 278528
  2576.3 189.7 %reduce-scatter.45.cloned.1.call-start = ((), (), s32[]{:S(2)}) async-start(), calls=%async_computation.39 | async-start | bytes 278528
  2580.1 187.3 %reduce-scatter.29.cloned.1.call-start = ((), (), s32[]{:S(2)}) async-start(), calls=%async_computation.31 | async-start | bytes 1114112 | tf_op jit(solution)/shard_map/reduce_scatter | solution.py:307
  2593.5 217.5 %reduce-scatter.27.cloned.1.call-start = ((), (), s32[]{:S(2)}) async-start(), calls=%async_computation.30 | async-start | bytes 1114112 | tf_op jit(solution)/shard_map/reduce_scatter | solution.py:304
  2631.2 244.1 %reduce-scatter.35.cloned.1.call-start = ((), (), s32[]{:S(2)}) async-start(), calls=%async_computation.34 | async-start | bytes 2228224 | tf_op jit(solution)/shard_map/reduce_scatter | solution.py:322
  2662.3 277.7 %reduce-scatter.31.cloned.1.call-start = ((), (), s32[]{:S(2)}) async-start(), calls=%async_computation.32 | async-start | bytes 2228224 | tf_op jit(solution)/shard_map/reduce_scatter | solution.py:310
  2700.9 303.4 %reduce-scatter.33.cloned.1.call-start = ((), (), s32[]{:S(2)}) async-start(), calls=%async_computation.33 | async-start | bytes 2228224 | tf_op jit(solution)/shard_map/reduce_scatter | solution.py:313
  2713.2 347.3 %reduce-scatter.25.cloned.1.call-start = ((), (), s32[]{:S(2)}) async-start(), calls=%async_computation.29 | async-start | bytes 6291456 | tf_op jit(solution)/shard_map/reduce_scatter | solution.py:289
  (708 other events, 9712.5 us)
Sparse Core Ops, SparseCore 0:
  10.2 40.6 all-gather.20
  53.0 55.6 all-gather.14
  150.9 40.2 all-gather.18
  193.3 40.1 all-gather.22
  656.8 98.1 reduce-scatter.18
  757.5 44.3 all-gather.28
  804.1 55.0 all-gather.26
  861.6 44.3 all-gather.30
  908.5 42.6 all-gather.32
  962.8 54.0 reduce-scatter.20
  1023.4 56.5 all-gather.34
  1117.1 54.2 reduce-scatter.22
  1183.9 56.7 all-gather.36
  1244.8 65.0 reduce-scatter.40
  1313.6 63.9 reduce-scatter.36
  1381.8 63.8 reduce-scatter.38
  2576.4 55.6 reduce-scatter.42
  2636.1 54.2 reduce-scatter.44
  2694.0 56.4 reduce-scatter.28
  2754.5 56.4 reduce-scatter.26
  2814.8 60.4 reduce-scatter.34
  2879.4 60.5 reduce-scatter.30
  2943.8 60.5 reduce-scatter.32
  3007.1 53.2 reduce-scatter.24
  (2 shorter events, 78.0 us)
where the time goes:
time: 3140 us; the launch traced here: 3120 us
  matrix products  1220 us (39%)
  waiting for transfers between devices  754 us (24%)
  local copies, waits for them, and re-layouts  576 us (18%)
  other arithmetic  386 us (12%)
  blocking collectives  122 us (4%)
  loops' own time  42.1 us (1%)
    dot_general x320, matrix products, lower_inverse(): power = jnp.einsum('hij,hjk->hik', power, power, precision=exact_precision)  163 us
    dot_general x320, matrix products, lower_inverse(): jnp.einsum('hij,hjk->hik', inverse, power, precision=exact_precision)  154 us
    squeeze x128, local copies, waits for them, and re-layouts, mixer_sequence(): lax.scan(jax.checkpoint(block_update), state, carried_in)  152 us
    dot_general x64, matrix products, block_update(): jnp.einsum('ihd,hde->ihe', keys, state, precision=exact_precision)  134 us
    dot_general x64, matrix products, block_update(): jnp.einsum('ihd,hde->ihe', queries, state, precision=exact_precision)  108 us
    reduce_scatter x1, waiting for transfers between devices, on_device(): lax.psum_scatter(contract_cols(mixed_low, full_out), 'tensor', scatter_di...  97.5 us
    dot_general x64, matrix products, block_update(): jnp.einsum('hij,jhe->hie', inverse, target_rows, precision=exact_precision)  91.9 us
    dot_general x10, matrix products, contract_cols(): lax.dot_general(left, right, (((1,), (1,)), ((), ())), preferred_element_...  87.2 us
  transfers between devices with their start and end apart: 26, of which 15 were waited for; matrix products, arithmetic and copies ran while one was open for 65% of the time, Pallas kernels for 0%

commit v1 on v0

--- a/solution.py
+++ b/solution.py
@@ -254,7 +254,7 @@
     live = pad_mask.astype(jnp.float32)
     error = output - target.astype(jnp.float32)
     loss_sum, count = lax.psum(
-        (jnp.sum(live[:, None] * error * error), jnp.sum(live)), ("dp", "tensor")
+        lax.psum((jnp.sum(live[:, None] * error * error), jnp.sum(live)), "tensor"), "dp"
     )
     loss = loss_sum / (count * width)
     all_tokens = own_rows * lax.axis_size("dp") * lax.axis_size("tensor")

time: 3140 us -> 3270 us (1.041)
  waiting for transfers between devices: 754 us -> 910 us
  blocking collectives: 122 us -> 78.7 us
    psum x0 -> x1, waiting for transfers between devices: none -> 121 us  [on_device(): lax.psum((grad_gain_one, grad_gain_two, conv_q_full, conv_k_full, conv_v_...]
    psum x2, blocking collectives: 81 us -> 38.2 us  [the longest x1 32.6 us: on_device(): lax.psum(lax.psum((jnp.sum(live[:, None] * error * error), jnp.sum(live))...]
    reduce_scatter x1, waiting for transfers between devices: 12.3 us -> 51.5 us  [on_device(): lax.psum_scatter(contract_cols(hidden, ffn_down_w).astype(jnp.bfloat16),...]
  transfers between devices with their start and end apart: 26 -> 27, of which waited for: 15 -> 16; matrix products, arithmetic and copies ran while one was open for 65% -> 63% of each run, Pallas kernels for 0% -> 0%
where the time goes in v1:
time: 3270 us; the launch traced here: 3250 us
  matrix products  1220 us (37%)
  waiting for transfers between devices  910 us (28%)
  local copies, waits for them, and re-layouts  587 us (18%)
  other arithmetic  388 us (12%)
  blocking collectives  78.7 us (2%)
  loops' own time  42.1 us (1%)
    dot_general x320, matrix products, lower_inverse(): power = jnp.einsum('hij,hjk->hik', power, power, precision=exact_precision)  163 us
    dot_general x320, matrix products, lower_inverse(): jnp.einsum('hij,hjk->hik', inverse, power, precision=exact_precision)  154 us
    squeeze x128, local copies, waits for them, and re-layouts, mixer_sequence(): lax.scan(jax.checkpoint(block_update), state, carried_in)  152 us
    dot_general x64, matrix products, block_update(): jnp.einsum('ihd,hde->ihe', keys, state, precision=exact_precision)  134 us
    psum x1, waiting for transfers between devices, on_device(): lax.psum((grad_gain_one, grad_gain_two, conv_q_full, conv_k_full, conv_v_...  121 us
    dot_general x64, matrix products, block_update(): jnp.einsum('ihd,hde->ihe', queries, state, precision=exact_precision)  108 us
    reduce_scatter x1, waiting for transfers between devices, on_device(): lax.psum_scatter(contract_cols(mixed_low, full_out), 'tensor', scatter_di...  97.5 us
    dot_general x64, matrix products, block_update(): jnp.einsum('hij,jhe->hie', inverse, target_rows, precision=exact_precision)  91.8 us
  transfers between devices with their start and end apart: 27, of which 16 were waited for; matrix products, arithmetic and copies ran while one was open for 63% of the time, Pallas kernels for 0%

profile of v1, /device:TPU:0, one launch (start us, length us, event | category | flops | bytes accessed | tf_op | source)
XLA Modules:
  0.0 3245.8 jit_solution(7779879012395116374)
XLA Ops:
  17.5 23.1 all-gather
  60.5 48.3 %all-gather.15.cloned.1.call-done = bf16[2048,1024]{1,0:T(8,128)(2,1)} async-done(((bf16[1024,1024]{1,0:T(8,128)(2,1)}), bf16[2048,1024]{1,0:T(8,128)(2,1)}) %all-gather.15.cloned.1.call-update) | async-done | bytes 4194320 | tf_op jit(solution)/shard_map/all_gather | solution.py:179
  115.6 33.3 %all-gather.17.cloned.1.call-done = bf16[1024,512]{1,0:T(8,128)(2,1)} async-done(((bf16[64,512]{1,0:T(8,128)(2,1)}), bf16[1024,512]{1,0:T(8,128)(2,1)}) %all-gather.17.cloned.1.call-update) | async-done | bytes 1048592 | tf_op jit(solution)/shard_map/all_gather | solution.py:182
  267.8 323.8 %while.42 = (s32[]{:T(128)}, f32[2,4,128,256]{3,2,1,0:T(8,128)S(1)}, f32[16,2,64,4,256]{4,2,3,1,0:T(8,128)}, f32[16,2,4,128,256]{4,3,2,1,0:T(8,128)}, s32[16,2,6...) while((s32[]{:T(128)}, ...), condition=%wide.region_5.6_spmd.clone, body=%wide.region_3.5_spmd.clone.sunk | while | flops 1160541952 | bytes 16545918 | solution.py:122
  657.9 97.5 %reduce-scatter.19.cloned.1.call-done = f32[1024,1024]{1,0:T(8,128)} async-done(((f32[2048,1024]{1,0:T(8,128)}), f32[1024,1024]{1,0:T(8,128)}) %reduce-scatter.19.cloned.1.call-update) | async-done | bytes 4194320 | tf_op jit(solution)/shard_map/reduce_scatter | solution.py:234
  763.3 38.9 %all-gather.29.cloned.1.call-done = bf16[1024,1408]{1,0:T(8,128)(2,1)} async-done(((bf16[64,1408]{1,0:T(8,128)(2,1)}), bf16[1024,1408]{1,0:T(8,128)(2,1)}) %all-gather.29.cloned.1.call-update) | async-done | bytes 2883600 | tf_op jit(solution)/shard_map/all_gather | solution.py:241
  802.3 57.3 %all-gather.27.cloned.1.call-done = bf16[2048,1024]{1,0:T(8,128)(2,1)} async-done(((bf16[1024,1024]{1,0:T(8,128)(2,1)}), bf16[2048,1024]{1,0:T(8,128)(2,1)}) %all-gather.27.cloned.1.call-update) | async-done | bytes 4194320 | tf_op jit(solution)/shard_map/all_gather | solution.py:239
  871.5 34.8 %all-gather.31.cloned.1.call-done = bf16[1024,1408]{1,0:T(8,128)(2,1)} async-done(((bf16[64,1408]{1,0:T(8,128)(2,1)}), bf16[1024,1408]{1,0:T(8,128)(2,1)}) %all-gather.31.cloned.1.call-update) | async-done | bytes 2883600 | tf_op jit(solution)/shard_map/all_gather | solution.py:242
  921.2 30.5 all-gather.33.cloned.1.call-done
  964.3 51.5 %reduce-scatter.21.cloned.1.call-done = bf16[1024,1024]{1,0:T(8,128)(2,1)} async-done(((bf16[2048,1024]{1,0:T(8,128)(2,1)}), bf16[1024,1024]{1,0:T(8,128)(2,1)}) %reduce-scatter.21.cloned.1.call-update) | async-done | bytes 2097168 | tf_op jit(solution)/shard_map/reduce_scatter | solution.py:247
  1027.7 32.6 %all-reduce.37 = (f32[]{:T(128)}, f32[]{:T(128)}) all-reduce(f32[]{:T(128)} %get-tuple-element.882, f32[]{:T(128)} %get-tuple-element.883), channel_id=1, replica_groups=mesh['dp'=16,'tensor'=2] {'dp'}, use_global_device_ids=true, to_apply=%region_12.13 | all-reduce | flops 2 | bytes 16 | tf_op jit(solution)/shard_map/psum | solution.py:256
  1065.2 53.2 %all-gather.35.cloned.1.call-done = bf16[2048,1024]{1,0:T(8,128)(2,1)} async-done(((bf16[1024,1024]{1,0:T(8,128)(2,1)}), bf16[2048,1024]{1,0:T(8,128)(2,1)}) %all-gather.35.cloned.1.call-update) | async-done | bytes 4194320 | tf_op jit(solution)/shard_map/all_gather | solution.py:262
  1118.4 19.6 multiply_convert_fusion
  1155.4 54.4 %reduce-scatter.23.cloned.1.call-done = bf16[1024,1024]{1,0:T(8,128)(2,1)} async-done(((bf16[2048,1024]{1,0:T(8,128)(2,1)}), bf16[1024,1024]{1,0:T(8,128)(2,1)}) %reduce-scatter.23.cloned.1.call-update) | async-done | bytes 2097168 | tf_op jit(solution)/shard_map/reduce_scatter | solution.py:273
  1277.3 18.8 fusion.145
  1338.5 1162.0 %while.43 = (s32[]{:T(128)}, f32[2,4,128,256]{3,2,1,0:T(8,128)}, f32[16,2,64,4,128]{4,2,3,1,0:T(8,128)}, f32[16,2,64,4,128]{4,2,3,1,0:T(8,128)}, f32[16,2,64,4,2...) while((s32[]{:T(128)}, f32[2,4,128,256]{3,2,1,0:T(8,128)}, ...), condition=%wide.region_29.30_spmd.clone, body=%wide.region_19.29_spmd.clone.sunk | while | flops 3179373312 | bytes 74722920 | solution.py:122
  2571.4 28.8 multiply_reduce_fusion.18
  2667.7 25.0 multiply_reduce_fusion.8
  2807.4 40.1 %reduce-scatter.27.cloned.1.call-done = bf16[64,512]{1,0:T(8,128)(2,1)} async-done(((bf16[1024,512]{1,0:T(8,128)(2,1)}), bf16[64,512]{1,0:T(8,128)(2,1)}) %reduce-scatter.27.cloned.1.call-update) | async-done | bytes 65552 | tf_op jit(solution)/shard_map/reduce_scatter | solution.py:304
  2849.0 62.9 %reduce-scatter.35.cloned.1.call-done = bf16[64,1024]{1,0:T(8,128)(2,1)} async-done(((bf16[1024,1024]{1,0:T(8,128)(2,1)}), bf16[64,1024]{1,0:T(8,128)(2,1)}) %reduce-scatter.35.cloned.1.call-update) | async-done | bytes 131088 | tf_op jit(solution)/shard_map/reduce_scatter | solution.py:322
  2913.5 63.1 %reduce-scatter.31.cloned.1.call-done = bf16[64,1024]{1,0:T(8,128)(2,1)} async-done(((bf16[1024,1024]{1,0:T(8,128)(2,1)}), bf16[64,1024]{1,0:T(8,128)(2,1)}) %reduce-scatter.31.cloned.1.call-update) | async-done | bytes 131088 | tf_op jit(solution)/shard_map/reduce_scatter | solution.py:310
  2978.2 62.7 %reduce-scatter.33.cloned.1.call-done = bf16[64,1024]{1,0:T(8,128)(2,1)} async-done(((bf16[1024,1024]{1,0:T(8,128)(2,1)}), bf16[64,1024]{1,0:T(8,128)(2,1)}) %reduce-scatter.33.cloned.1.call-update) | async-done | bytes 131088 | tf_op jit(solution)/shard_map/reduce_scatter | solution.py:313
  3042.5 54.5 %reduce-scatter.25.cloned.1.call-done = bf16[1024,1024]{1,0:T(8,128)(2,1)} async-done(((bf16[2048,1024]{1,0:T(8,128)(2,1)}), bf16[1024,1024]{1,0:T(8,128)(2,1)}) %reduce-scatter.25.cloned.1.call-update) | async-done | bytes 2097168 | tf_op jit(solution)/shard_map/reduce_scatter | solution.py:289
  3105.8 121.4 %all-reduce.41.cloned.1.call-done = (f32[1024]{0:T(1024)}, f32[4,1024]{1,0:T(4,128)}, f32[4,1024]{1,0:T(4,128)}, f32[4,2048]{1,0:T(4,128)}, f32[8]{0:T(128)}, /*index=5*/f32[8]{0:T(128)}, f32[256]{0:T(256)}, f32[1024]{0:T(1024)}) async-done(((f32[1024]{0:T(1024)}, f32[4,1024]{1,0:T(4,128)}, f32[4,1024]{1,0:T(4,128)}, f32[4,2048]{1,0:T(4,128)}, f32[8]{0:T(128)}, /*index=5*/f32[8]{0:T(128)}, f32[256]{0:T(256)}, ...) | async-done | bytes 74832 | tf_op jit(solution)/shard_map/psum | solution.py:341
  (3589 shorter events, 2131.6 us)
Async XLA Ops:
  14.8 134.1 %all-gather.17.cloned.1.call-start = ((), (), s32[]{:S(2)}) async-start(), calls=%async_computation.15 | async-start | bytes 1114112 | tf_op jit(solution)/shard_map/all_gather | solution.py:182
  15.5 203.3 %all-gather.19.cloned.1.call-start = ((), (), s32[]{:S(2)}) async-start(), calls=%async_computation.16 | async-start | bytes 2228224 | tf_op jit(solution)/shard_map/all_gather | solution.py:183
  16.1 611.7 %all-gather.23.cloned.1.call-start = ((), (), s32[]{:S(2)}) async-start(), calls=%async_computation.18 | async-start | bytes 2228224 | tf_op jit(solution)/shard_map/all_gather | solution.py:184
  16.7 629.6 %all-gather.25.cloned.1.call-start = ((), (), s32[]{:S(2)}) async-start(), calls=%async_computation.19 | async-start | bytes 2228224 | tf_op jit(solution)/shard_map/all_gather | solution.py:187
  17.3 738.1 %reduce-scatter.19.cloned.1.call-start = ((), (), s32[]{:S(2)}) async-start(), calls=%async_computation.20 | async-start | bytes 12582912 | tf_op jit(solution)/shard_map/reduce_scatter | solution.py:234
  657.1 145.2 %all-gather.29.cloned.1.call-start = ((), (), s32[]{:S(2)}) async-start(), calls=%async_computation.22 | async-start | bytes 3063808 | tf_op jit(solution)/shard_map/all_gather | solution.py:241
  657.8 201.8 %all-gather.27.cloned.1.call-start = ((), (), s32[]{:S(2)}) async-start(), calls=%async_computation.21 | async-start | bytes 6291456 | tf_op jit(solution)/shard_map/all_gather | solution.py:239
  762.0 144.4 %all-gather.31.cloned.1.call-start = ((), (), s32[]{:S(2)}) async-start(), calls=%async_computation.23 | async-start | bytes 3063808 | tf_op jit(solution)/shard_map/all_gather | solution.py:242
  762.6 189.1 %all-gather.33.cloned.1.call-start = ((), (), s32[]{:S(2)}) async-start(), calls=%async_computation.24 | async-start | bytes 3063808 | tf_op jit(solution)/shard_map/all_gather | solution.py:243
  763.3 252.5 %reduce-scatter.21.cloned.1.call-start = ((), (), s32[]{:S(2)}) async-start(), calls=%async_computation.25 | async-start | bytes 6291456 | tf_op jit(solution)/shard_map/reduce_scatter | solution.py:247
  963.1 155.3 %all-gather.35.cloned.1.call-start = ((), (), s32[]{:S(2)}) async-start(), calls=%async_computation.26 | async-start | bytes 6291456 | tf_op jit(solution)/shard_map/all_gather | solution.py:262
  1065.1 144.6 %reduce-scatter.23.cloned.1.call-start = ((), (), s32[]{:S(2)}) async-start(), calls=%async_computation.27 | async-start | bytes 6291456 | tf_op jit(solution)/shard_map/reduce_scatter | solution.py:273
  1220.1 1575.0 %reduce-scatter.41.cloned.1.call-start = ((), (), s32[]{:S(2)}) async-start(), calls=%async_computation.37 | async-start | bytes 3063808 | tf_op jit(solution)/shard_map/reduce_scatter | solution.py:301
  1232.1 1564.7 %reduce-scatter.37.cloned.1.call-start = ((), (), s32[]{:S(2)}) async-start(), calls=%async_computation.35 | async-start | bytes 3063808 | tf_op jit(solution)/shard_map/reduce_scatter | solution.py:295
  1243.7 1554.8 %reduce-scatter.39.cloned.1.call-start = ((), (), s32[]{:S(2)}) async-start(), calls=%async_computation.36 | async-start | bytes 3063808 | tf_op jit(solution)/shard_map/reduce_scatter | solution.py:298
  1277.2 1526.0 %reduce-scatter.43.cloned.1.call-start = ((), (), s32[]{:S(2)}) async-start(), calls=%async_computation.38 | async-start | bytes 278528
  2612.7 191.8 %reduce-scatter.45.cloned.1.call-start = ((), (), s32[]{:S(2)}) async-start(), calls=%async_computation.39 | async-start | bytes 278528
  2616.5 189.4 %reduce-scatter.29.cloned.1.call-start = ((), (), s32[]{:S(2)}) async-start(), calls=%async_computation.31 | async-start | bytes 1114112 | tf_op jit(solution)/shard_map/reduce_scatter | solution.py:307
  2629.9 217.6 %reduce-scatter.27.cloned.1.call-start = ((), (), s32[]{:S(2)}) async-start(), calls=%async_computation.30 | async-start | bytes 1114112 | tf_op jit(solution)/shard_map/reduce_scatter | solution.py:304
  2667.6 244.3 %reduce-scatter.35.cloned.1.call-start = ((), (), s32[]{:S(2)}) async-start(), calls=%async_computation.34 | async-start | bytes 2228224 | tf_op jit(solution)/shard_map/reduce_scatter | solution.py:322
  2698.5 278.1 %reduce-scatter.31.cloned.1.call-start = ((), (), s32[]{:S(2)}) async-start(), calls=%async_computation.32 | async-start | bytes 2228224 | tf_op jit(solution)/shard_map/reduce_scatter | solution.py:310
  2737.2 303.7 %reduce-scatter.33.cloned.1.call-start = ((), (), s32[]{:S(2)}) async-start(), calls=%async_computation.33 | async-start | bytes 2228224 | tf_op jit(solution)/shard_map/reduce_scatter | solution.py:313
  2749.5 347.6 %reduce-scatter.25.cloned.1.call-start = ((), (), s32[]{:S(2)}) async-start(), calls=%async_computation.29 | async-start | bytes 6291456 | tf_op jit(solution)/shard_map/reduce_scatter | solution.py:289
  2793.5 433.6 %all-reduce.41.cloned.1.call-start = ((), (), s32[]{:S(2)}) async-start(), calls=%async_computation.40 | async-start | bytes 151552 | tf_op jit(solution)/shard_map/psum | solution.py:341
  (711 other events, 10717.3 us)
Sparse Core Ops, SparseCore 0:
  10.2 40.6 all-gather.20
  53.0 55.6 all-gather.14
  150.9 40.3 all-gather.18
  657.2 98.1 reduce-scatter.18
  757.9 44.3 all-gather.28
  804.5 55.0 all-gather.26
  862.0 44.3 all-gather.30
  908.9 42.6 all-gather.32
  963.2 52.6 reduce-scatter.20
  1065.3 53.0 all-gather.34
  1155.5 54.2 reduce-scatter.22
  1220.2 56.7 all-gather.36
  1281.2 65.0 reduce-scatter.40
  1349.9 63.8 reduce-scatter.36
  1417.9 64.1 reduce-scatter.38
  2612.8 55.6 reduce-scatter.42
  2672.5 54.3 reduce-scatter.44
  2730.5 56.4 reduce-scatter.28
  2791.0 56.5 reduce-scatter.26
  2851.3 60.5 reduce-scatter.34
  2915.9 60.5 reduce-scatter.30
  2980.3 60.5 reduce-scatter.32
  3043.7 53.2 reduce-scatter.24
  3105.1 122.0 all-reduce.40
  (3 shorter events, 118.2 us)
